TPU v7x, 128 devices: a whole 4x4x4 slice. The times are simulated.
128 devices in a mesh: tile: 16 (over x_lo, z, core), chan: 8 (over y, x_hi).
Axes of the slice: x: 4 (x_hi: 2, x_lo: 2; x = x_hi * 2 + x_lo), y: 4, z: 4, core: 2. Of those that a mesh axis runs over, the one named last changes fastest.
Arguments:
- voltages: int32 [512, 262144], P('tile', 'chan'), may hold values from -128 to 127
- history: int32 [512, 30720], P('tile'), may hold values from -128 to 127
- filter_taps: int32 [16, 2048], replicated, may hold values from -64 to 64
Outputs:
- visibilities: float32 [2, 1024, 512, 512], P(None, 'chan', 'tile')
Inputs may be any that keep to these rules, and one draw needn't show every extreme that they name: `voltages`: 8-bit signed samples. `history`: 8-bit signed samples.
All inputs are finite; a program needn't handle non-finite values.
Results may differ from a plain program's by a relative error of at most 0.006.
Values may be sent and summed in bfloat16 or wider, within the bound.
A program may use at most 192 MiB of HBM per device.

v0:
```python
import math

import jax
import jax.numpy as jnp
from jax import lax
from jax.sharding import PartitionSpec as P

CH = 1024
TAPS = 16
FFT = 2048


filter_norm = 1.0 / 16384.0


def from_behind(value, axis, steps):
    count = lax.axis_size(axis)
    leading, last = (max(0, -steps), min(count, count - steps))
    return lax.ppermute(value, axis, [(source, source + steps) for source in range(leading, last)])


def dft_table(samples, channels):
    rows_index = jnp.arange(samples, dtype=jnp.int32)[:, None]
    cols_index = jnp.arange(channels, dtype=jnp.int32)[None, :]
    angles = (rows_index * cols_index % samples).astype(jnp.float32) * (2.0 * math.pi / samples)
    factor = 1.0 / math.sqrt(channels)
    return jnp.concatenate([jnp.cos(angles) * factor, -jnp.sin(angles) * factor], axis=1).astype(
        jnp.bfloat16
    )


def polyphase(extended, weights, spectra_count):
    summed = jnp.zeros((extended.shape[0], spectra_count, extended.shape[2]), jnp.float32)
    for tap_index in range(weights.shape[0]):
        summed = (
            summed
            + weights[tap_index][None, None, :]
            * extended[:, tap_index : tap_index + spectra_count, :]
        )
    return summed


def counter_rows(spectra):
    real_part = spectra[:, :, 0]
    imag_part = spectra[:, :, 1]
    rotated = jnp.stack([imag_part, -real_part], axis=2)
    return jnp.stack([spectra, rotated], axis=0)


def body(voltages, history, filter_taps):
    local_inputs = voltages.shape[0]
    spectra_count = voltages.shape[1] // FFT
    tail_blocks = voltages[:, (spectra_count - TAPS + 1) * FFT :].astype(jnp.bfloat16)
    carried = from_behind(tail_blocks, "chan", 1)
    is_first = lax.axis_index("chan") == 0
    earlier = jnp.where(is_first, history.astype(jnp.float32), carried.astype(jnp.float32))
    extended = jnp.concatenate([earlier, voltages.astype(jnp.float32)], axis=1)
    extended = extended.reshape(local_inputs, spectra_count + TAPS - 1, FFT)
    filtered = (
        polyphase(extended, filter_taps.astype(jnp.float32), spectra_count) * filter_norm
    ).astype(jnp.bfloat16)
    spectra = jnp.dot(
        filtered.reshape(-1, FFT), dft_table(FFT, CH), preferred_element_type=jnp.float32
    )
    spectra = spectra.reshape(local_inputs, spectra_count, 2, CH).astype(jnp.bfloat16)
    turned = lax.all_to_all(spectra, "chan", split_axis=3, concat_axis=1, tiled=True)
    total_spectra = turned.shape[1]
    average = 1.0 / total_spectra
    row_sets = counter_rows(turned)
    return (
        jnp.einsum(
            "qaspc,bspc->qcab",
            row_sets,
            lax.all_gather(turned, "tile", axis=0, tiled=True),
            preferred_element_type=jnp.float32,
        )
        * average
    )


def solution(mesh):
    in_specs = (P("tile", "chan"), P("tile", None), P())
    out_specs = P(None, "chan", "tile", None)
    return jax.shard_map(body, mesh=mesh, in_specs=in_specs, out_specs=out_specs, check_vma=False)
```

profile of v0, /device:TPU:1, one launch (start us, length us, event | category | flops | bytes accessed | tf_op | source)
XLA Modules:
  0.0 409.3 jit_solution(11984337973401259222)
XLA Ops:
  6.5 0.0 copy-start.3
  6.5 0.0 all-gather.2.cloned.1.call-start
  6.5 0.0 copy-start.1
  6.5 3.7 slice_convert_fusion
  10.3 5.6 %collective-permute-start = (bf16[32,30720]{1,0:T(8,128)(2,1)}, bf16[32,30720]{1,0:T(8,128)(2,1)S(1)}, u32[]{:S(2)}, u32[]{:S(2)}) collective-permute-start(bf16[32,30720]{1,0:T(8,128)(2,1)} %slice_convert_fusion), channel_id=1, source_target_pairs={{0,1},{1,2},{2,3},{3,4},{4,5},{5,6},{6,7},{8,9},{9,10},{10,11},{11... | collective-permute-start | bytes 5898248 | tf_op jit(solution)/shard_map/ppermute | solution.py:19
  15.9 0.0 copy-done.3
  15.9 0.1 fusion.40
  16.0 0.0 copy-done.1
  16.0 2.2 convert_element_type.28
  18.2 34.9 %multiply_convert_fusion = (bf16[2048,1024]{0,1:T(8,128)(2,1)}, bf16[2048,1024]{0,1:T(8,128)(2,1)}) fusion(), kind=kLoop, calls=%fused_computation.11 | loop fusion | flops 39845888 | bytes 8388608 | tf_op jit(solution)/shard_map/convert.1
  53.2 8.5 %pad_maximum_fusion = bf16[2048,2048]{0,1:T(8,128)(2,1)} fusion(bf16[2048,1024]{0,1:T(8,128)(2,1)} %get-tuple-element.23, bf16[2048,1024]{0,1:T(8,128)(2,1)} %get-tuple-element.24), kind=kLoop, calls=%fused_computation.10 | loop fusion | flops 16777216 | bytes 16777216 | tf_op jit(solution)/shard_map/concatenate | solution.py:27
  61.7 0.0 copy-start
  61.7 0.0 collective-permute-done
  61.7 2.6 convert_select_fusion
  64.4 0.7 copy-done
  65.1 3.7 pad_maximum_fusion.1
  68.7 7.6 %reshape.25 = f32[32,31,2048]{2,1,0:T(8,128)} reshape(f32[32,63488]{1,0:T(8,128)} %pad_maximum_fusion.1) | data formatting | bytes 16252928 | tf_op jit(solution)/shard_map/reshape | solution.py:58
  76.4 43.5 %fusion.34 = bf16[32,16,2,1024]{3,1,2,0:T(8,128)(2,1)S(1)} fusion(bf16[2,1024,2048,1]{2,1,0,3:T(8,128)(2,1)} %bitcast.59, f32[32,31,2048]{2,1,0:T(8,128)} %reshape.25, f32[2048]{0:T(1024)S(1)} %bitcast.61, f32[2048]{0:T(1024)S(1)} %bitcast.62, f32[2048]{0:T(1024)S(1)} %bitcast.63, f32[2048]{0:T(1024)S(1)} %bitcast.64, f32[2048]{0:T(1024)S(1)} %bitcast.65, ...), kind=kOutput, calls=%fused_computation.58 | convolution fusion | flops 4330618880 | bytes 77725696 | tf_op jit(solution)/shard_map/dot_general | solution.py:62
  119.9 12.8 %copy.28 = bf16[32,16,2,1024]{0,1,2,3:T(8,128)(2,1)} copy(bf16[32,16,2,1024]{3,1,2,0:T(8,128)(2,1)S(1)} %fusion.34) | data formatting | bytes 4194304 | tf_op jit(solution)/shard_map/convert_element_type | solution.py:65
  132.7 10.1 %reshape.30 = bf16[8,2,65536]{2,1,0:T(2,128)(2,1)S(1)} reshape(bf16[1024,2,16,32]{3,2,1,0:T(8,128)(2,1)} %bitcast.55) | data formatting | bytes 4194304
  142.9 31.9 %all_to_all.18 = bf16[8,2,65536]{2,1,0:T(2,128)(2,1)} all-to-all(bf16[8,2,65536]{2,1,0:T(2,128)(2,1)S(1)} %reshape.30), channel_id=1, replica_groups=mesh['tile'=16,'chan'=8] {'chan'}, dimensions={0} | all-to-all | bytes 4194304 | tf_op jit(solution)/shard_map/all_to_all | solution.py:66
  174.8 8.6 %reshape.31 = bf16[1024,2,16,32]{3,2,1,0:T(8,128)(2,1)} reshape(bf16[8,2,65536]{2,1,0:T(2,128)(2,1)} %all_to_all.18) | data formatting | bytes 4194304
  183.4 10.3 %copy.30 = bf16[32,8,16,2,128]{4,2,1,3,0:T(8,128)(2,1)S(1)} copy(bf16[32,8,16,2,128]{0,2,3,4,1:T(8,128)(2,1)} %bitcast.56) | data formatting | bytes 4194304 | tf_op jit(solution)/shard_map/all_to_all | solution.py:66
  193.7 2.9 copy.31
  196.6 0.0 all-gather.2.cloned.1.call-update
  196.6 3.0 copy.35
  199.6 0.0 copy-start.2
  199.6 1.9 fusion.39
  201.5 1.5 maximum_bitcast_fusion
  203.1 165.1 %all-gather.2.cloned.1.call-done = bf16[512,128,2,128]{1,0,2,3:T(8,128)(2,1)} async-done(((bf16[32,128,2,128]{1,0,2,3:T(8,128)(2,1)}), bf16[512,128,2,128]{1,0,2,3:T(8,128)(2,1)}) %all-gather.2.cloned.1.call-update) | async-done | bytes 33554448 | tf_op jit(solution)/shard_map/all_gather | solution.py:74
  368.1 0.0 copy-done.2
  368.1 21.9 %fusion.2 = f32[2,128,32,512]{3,2,0,1:T(8,128)} fusion(bf16[512,128,2,128]{1,0,2,3:T(8,128)(2,1)} %all-gather.2.cloned.1.call-done, bf16[1,32,128,2,128]{2,1,3,0,4:T(8,128)(2,1)} %maximum_bitcast_fusion, bf16[1,32,128,2,128]{2,1,3,0,4:T(8,128)(2,1)S(1)} %copy-done.2), kind=kOutput, calls=%fused_computation.3 | convolution fusion | flops 2160066560 | bytes 54525952 | tf_op jit(solution)/shard_map/qaspc,bspc->qcab/dot_general | solution.py:71
  390.1 12.4 %copy.36 = f32[2,128,32,512]{3,2,1,0:T(8,128)} copy(f32[2,128,32,512]{3,2,0,1:T(8,128)} %fusion.2) | data formatting | bytes 33554432 | tf_op jit(solution)/shard_map/mul | solution.py:71
  (1 shorter events, 0.0 us)
Async XLA Ops:
  6.5 9.3 %copy-start.3 = (s32[16,2048]{1,0:T(8,128)S(1)}, s32[16,2048]{1,0:T(8,128)}, u32[]{:S(2)}) copy-start(s32[16,2048]{1,0:T(8,128)} %param.5) | copy-start | bytes 393220
  6.5 361.6 %all-gather.2.cloned.1.call-start = ((), (), s32[]{:S(2)}) async-start(), calls=%async_computation.1 | async-start | bytes 35651584 | tf_op jit(solution)/shard_map/all_gather | solution.py:74
  6.5 9.5 %copy-start.1 = (s32[32,32768]{1,0:T(8,128)S(1)}, s32[32,32768]{1,0:T(8,128)}, u32[]{:S(2)}) copy-start(s32[32,32768]{1,0:T(8,128)} %param.3) | copy-start | bytes 12582916
  10.3 51.4 %collective-permute-start = (bf16[32,30720]{1,0:T(8,128)(2,1)}, bf16[32,30720]{1,0:T(8,128)(2,1)S(1)}, u32[]{:S(2)}, u32[]{:S(2)}) collective-permute-start(bf16[32,30720]{1,0:T(8,128)(2,1)} %slice_convert_fusion), channel_id=1, source_target_pairs={{0,1},{1,2},{2,3},{3,4},{4,5},{5,6},{6,7},{8,9},{9,10},{10,11},{11... | collective-permute-start | bytes 5898248 | tf_op jit(solution)/shard_map/ppermute | solution.py:19
  61.7 3.4 copy-start
  199.6 168.5 %copy-start.2 = (bf16[1,32,128,2,128]{2,1,3,0,4:T(8,128)(2,1)S(1)}, bf16[1,32,128,2,128]{2,1,3,0,4:T(8,128)(2,1)}, u32[]{:S(2)}) copy-start(bf16[1,32,128,2,128]{2,1,3,0,4:T(8,128)(2,1)} %copy.35) | copy-start | bytes 6291460
Sparse Core Ops, SparseCore 0:
  196.8 171.3 all-gather.1
where the time goes:
time: 410 us; the launch traced here: 409 us
  waiting for transfers between devices  165 us (40%)
  local copies, waits for them, and re-layouts  68.6 us (17%)
  matrix products  65.5 us (16%)
  other arithmetic  59.2 us (14%)
  blocking collectives  31.9 us (8%)
  between operations  13.5 us (3%)
  starting transfers between devices  5.58 us (1%)
    all_gather x1, waiting for transfers between devices, body(): lax.all_gather(turned, 'tile', axis=0, tiled=True)  165 us
    dot_general x1, matrix products, body(): jnp.dot(filtered.reshape(-1, FFT), dft_table(FFT, CH), preferred_element_...  43.5 us
    another operation x2, other arithmetic  38.7 us
    all_to_all x1, blocking collectives, body(): lax.all_to_all(spectra, 'chan', split_axis=3, concat_axis=1, tiled=True)  31.9 us
    dot_general x1, matrix products, body(): jnp.einsum('qaspc,bspc->qcab', row_sets, lax.all_gather(turned, 'tile', a...  21.9 us
    unnamed x10, local copies, waits for them, and re-layouts  19.5 us
    all_to_all x2, local copies, waits for them, and re-layouts, body(): lax.all_to_all(spectra, 'chan', split_axis=3, concat_axis=1, tiled=True)  13.2 us
    convert_element_type x1, local copies, waits for them, and re-layouts, body(): spectra.reshape(local_inputs, spectra_count, 2, CH).astype(jnp.bfloat16)  12.8 us
  transfers between devices with their start and end apart: 2, of which 1 were waited for; matrix products, arithmetic and copies ran while one was open for 13% of the time, Pallas kernels for 0%

commit v1 on v0

v1 whole, which is shorter than its diff:
```python
import functools
import math

import jax
import jax.numpy as jnp
import numpy as np
from jax import lax
from jax.experimental import pallas as pl
from jax.experimental.pallas import tpu as pltpu
from jax.sharding import PartitionSpec as P

CH = 1024
TAPS = 16
FFT = 2048
SPEC = 128
INPUTS = 512

NT = FFT // 128
CHAN = 8
ROWS = 32
OWN = ROWS // CHAN
SLOC = SPEC // CHAN
KD = 32
CK = 4
NCH = KD // CK
AHEAD = 2

MESH = pl.DeviceIdType.MESH
F32 = jnp.float32
BF16 = jnp.bfloat16


def phase_tables():
    k = np.arange(CH, dtype=np.int64)
    fine = (k[:, None] * np.arange(128)[None, :]) % FFT * (2.0 * math.pi / FFT)
    fine = np.stack([np.cos(fine), np.sin(fine)]) / math.sqrt(CH)
    coarse = (np.arange(NT)[:, None] * np.arange(16)[None, :]) % 16 * (2.0 * math.pi / 16)
    coarse = np.stack([np.cos(coarse), np.sin(coarse)])
    coarse = np.broadcast_to(coarse[..., None], (2, NT, 16, 128))
    return fine.astype(np.float32), np.ascontiguousarray(coarse).astype(np.float32)


def place():
    tile, chan = lax.axis_index("tile"), lax.axis_index("chan")
    x_lo, z, core = tile // 8, (tile // 2) % 4, tile % 2
    return tile, chan, x_lo, z, core


def plane_tile(q, z):
    return (q // 2) * 8 + z * 2 + q % 2


def front_kernel(
    volt, hist, taps, fine, coarse, got,
    h8, table, pack, hpack, send, recv, ext, filt, fir, spec, out2,
    hsem, s1, r1, s2, r2, lsem,
):
    tile, chan, x_lo, z, core = place()
    q = x_lo * 2 + core
    hcopy = pltpu.make_async_copy(
        hist.at[pl.ds(pl.multiple_of((chan // 2) * 8, 8), 8), :], h8, hsem
    )
    hcopy.start()

    barrier = pltpu.get_barrier_semaphore()

    @pl.loop(1, 32)
    def _(i):
        other = lax.rem(q * 8 + chan + i, 32)
        pl.semaphore_signal(
            barrier, inc=1, device_id=(plane_tile(other // 8, z), other % 8), device_id_type=MESH
        )

    @pl.loop(0, NT)
    def _(nt):
        for s in range(SLOC):
            lanes = pl.ds(pl.multiple_of(s * FFT + nt * 128, 128), 128)
            pack[pl.ds(s, ROWS, stride=SLOC), :] = volt[:, lanes].astype(F32)
        for c in range(CHAN):
            send[c, nt] = pack[pl.ds(c * OWN * SLOC, OWN * SLOC), :].astype(BF16)

    pl.semaphore_wait(barrier, 31)

    def first(i):
        to = lax.rem(chan + i, CHAN)
        return pltpu.make_async_remote_copy(
            src_ref=send.at[to], dst_ref=recv.at[chan], send_sem=s1.at[to], recv_sem=r1.at[chan],
            device_id=(tile, to), device_id_type=MESH,
        )

    def first_in(i):
        src = lax.rem(chan + CHAN - i, CHAN)
        return pltpu.make_async_remote_copy(
            src_ref=send.at[src], dst_ref=recv.at[src], send_sem=s1.at[src], recv_sem=r1.at[src],
            device_id=(tile, src), device_id_type=MESH,
        )

    @pl.loop(1, CHAN)
    def _(i):
        first(i).start()

    recv[chan] = send[chan]
    hcopy.wait()

    @pl.loop(0, CH // 16)
    def _(kb):
        rows = pl.ds(pl.multiple_of(kb * 16, 16), 16)
        rows_im = pl.ds(pl.multiple_of(CH + kb * 16, 16), 16)
        c2, s2_ = fine[0, rows, :], fine[1, rows, :]
        for n1 in range(NT):
            c1, s1_ = coarse[0, n1], coarse[1, n1]
            lanes = pl.ds(n1 * 128, 128)
            table[rows, lanes] = (c1 * c2 - s1_ * s2_).astype(BF16)
            table[rows_im, lanes] = (-(s1_ * c2 + c1 * s2_)).astype(BF16)

    @pl.loop(1, CHAN)
    def _(i):
        first_in(i).wait_recv()

    odd = lax.rem(chan, 2)

    @pl.loop(0, NT)
    def _(nt):
        for j in range(TAPS - 1):
            lanes = pl.ds(pl.multiple_of(j * FFT + nt * 128, 128), 128)
            hpack[pl.ds(j + 1, 8, stride=16), :] = h8[:, lanes].astype(F32)
        for a in range(OWN):
            old = hpack[pl.ds(pl.multiple_of(odd * 64 + a * 16, 16), 16), :]
            ext[pl.ds(a * 2, 16, stride=8), :] = old
        for c in range(CHAN):
            for a in range(OWN):
                part = recv[c, nt, a * 16 : (a + 1) * 16, :].astype(F32)
                start = (16 + (c % 4) * 16) * 8 + a * 2 + c // 4
                ext[pl.ds(start, 16, stride=8), :] = part
                if c == 3:
                    ext[pl.ds(a * 2 + 1, 16, stride=8), :] = part
        lanes = pl.ds(pl.multiple_of(nt * 128, 128), 128)
        weights = [
            jnp.broadcast_to(taps[t : t + 1, lanes].astype(F32), (8, 128)) for t in range(TAPS)
        ]

        @pl.loop(0, 64, step=8)
        def _(j0):
            base = pl.multiple_of(j0 * 8, 64)
            rows = [ext[pl.ds(base + (r + 1) * 8, 8), :] for r in range(8 + TAPS - 1)]
            for j in range(8):
                total = weights[0] * rows[j]
                for t in range(1, TAPS):
                    total = total + weights[t] * rows[j + t]
                fir[pl.ds(j0 + j, 8, stride=64), :] = total * (1.0 / 16384.0)

        filt[:, lanes] = fir[...].astype(BF16)

    def second(i, m, kb):
        to = lax.rem(q + m, 4)
        return pltpu.make_async_remote_copy(
            src_ref=out2.at[kb, to], dst_ref=got.at[q, chan],
            send_sem=s2.at[kb, to], recv_sem=r2.at[q, chan],
            device_id=(plane_tile(to, z), kb), device_id_type=MESH,
        )

    own = pltpu.make_async_copy(out2.at[chan, q], got.at[q, chan], lsem)

    @pl.loop(0, CHAN)
    def _(i):
        kb = lax.rem(chan + 1 + i, CHAN)
        for p in range(2):
            rows = pl.ds(pl.multiple_of(p * CH + kb * 128, 128), 128)
            block = lax.dot_general(
                table[rows, :], filt[...], (((1,), (1,)), ((), ())), preferred_element_type=F32
            )
            for a in range(OWN):
                spec[pl.ds(p * OWN + a, 128, stride=8), :] = block[:, a * 128 : (a + 1) * 128]
        for to in range(4):
            out2[kb, to] = spec[pl.ds(to * 256, 256), :].astype(BF16)

        for m in (1, 2, 3):
            second(i, m, kb).start()

        @pl.when(i < CHAN - 1)
        def _():
            second(i, 0, kb).start()

    own.start()

    @pl.loop(1, CHAN)
    def _(i):
        first(i).wait_send()

    @pl.loop(1, 32)
    def _(i):
        other = lax.rem(q * 8 + chan + i, 32)
        oq, oc = other // 8, other % 8
        copy = pltpu.make_async_remote_copy(
            src_ref=out2.at[oc, oq], dst_ref=got.at[oq, oc],
            send_sem=s2.at[oc, oq], recv_sem=r2.at[oq, oc],
            device_id=(plane_tile(oq, z), oc), device_id_type=MESH,
        )
        copy.wait_send()
        copy.wait_recv()

    own.wait()


def back_kernel(
    got, out, gather, ob, sz, rz, so, ro, lsem,
):
    tile, chan, x_lo, z, core = place()
    q = x_lo * 2 + core
    up, down = lax.rem(z + 1, 4), lax.rem(z + 3, 4)
    far = lax.rem(z + 2, 4)

    barrier = pltpu.get_barrier_semaphore()
    for nz in (up, down):
        pl.semaphore_signal(
            barrier, inc=1, device_id=(plane_tile(q, nz), chan), device_id_type=MESH
        )
    for m in (1, 2, 3):
        to = lax.rem(q + m, 4)
        pl.semaphore_signal(
            barrier, inc=1, device_id=(plane_tile(to, z), chan), device_id_type=MESH
        )

    low = lax.broadcasted_iota(jnp.int32, (8, 128), 0) < 4

    @pl.loop(0, KD // 2)
    def _(kp):
        rows = pl.ds(pl.multiple_of(kp * 16, 16), 16)
        for member in range(4):
            mx, mc = member // 2, member % 2
            for half in range(2):
                parts = [got[member, half * 4 + c, rows, :].astype(F32) for c in range(4)]
                for kk in range(2):
                    v = [part[kk * 8 : kk * 8 + 8, :] for part in parts]
                    r = [pltpu.roll(x, 4, 0) for x in v]
                    re = jnp.concatenate(
                        [jnp.where(low, v[0], r[1]), jnp.where(low, v[2], r[3])], axis=0
                    )
                    im = jnp.concatenate(
                        [jnp.where(low, r[0], v[1]), jnp.where(low, r[2], v[3])], axis=0
                    )
                    at = pl.ds(mc * 32 + half * 16, 16)
                    gather[kp * 2 + kk, mx, z, at, 0:128] = re.astype(BF16)
                    gather[kp * 2 + kk, mx, z, at, 128:256] = im.astype(BF16)

    pl.semaphore_wait(barrier, 5)

    def shift(chunk, owner, to, way):
        block = gather.at[pl.ds(chunk * CK, CK), :, owner]
        return pltpu.make_async_remote_copy(
            src_ref=block, dst_ref=block, send_sem=sz.at[way, chunk], recv_sem=rz.at[way, chunk],
            device_id=(plane_tile(q, to), chan), device_id_type=MESH,
        )

    def spread(chunk, m):
        to = lax.rem(q + m, 4)
        return pltpu.make_async_remote_copy(
            src_ref=ob.at[to, :, pl.ds(chunk * CK, CK)],
            dst_ref=out.at[:, q, pl.ds(chunk * CK, CK)],
            send_sem=so.at[to, chunk], recv_sem=ro.at[q, chunk],
            device_id=(plane_tile(to, z), chan), device_id_type=MESH,
        )

    def keep(chunk):
        return pltpu.make_async_copy(
            ob.at[q, :, pl.ds(chunk * CK, CK)], out.at[:, q, pl.ds(chunk * CK, CK)],
            lsem.at[chunk],
        )

    def start_own(chunk):
        shift(chunk, z, up, 0).start()
        shift(chunk, z, down, 1).start()

    for chunk in range(AHEAD):
        start_own(chunk)

    @pl.loop(0, NCH + 1)
    def _(step):
        @pl.when(step + AHEAD < NCH)
        def _():
            start_own(step + AHEAD)

        @pl.when(step < NCH)
        def _():
            shift(step, down, up, 0).wait_recv()
            shift(step, up, down, 1).wait_recv()

            @pl.when(lax.rem(step, 2) == 0)
            def _():
                shift(step, down, up, 2).start()

            @pl.when(lax.rem(step, 2) == 1)
            def _():
                shift(step, up, down, 2).start()

        @pl.when(step > 0)
        def _():
            chunk = step - 1
            shift(chunk, far, up, 2).wait_recv()

            @pl.loop(chunk * CK, chunk * CK + CK)
            def _(k):
                mine = gather[k, :, z].reshape(128, 256)
                re, im = mine[:, :128], mine[:, 128:]
                turned = jnp.concatenate([im, -re], axis=1)
                left = jnp.concatenate([mine, turned], axis=0)
                right = gather[k].reshape(INPUTS, 256)
                vis = lax.dot_general(
                    left, right, (((1,), (1,)), ((), ())), preferred_element_type=F32
                )
                vis = (vis * (1.0 / SPEC)).astype(BF16)
                for to in range(4):
                    for p in range(2):
                        ob[to, p, k] = vis[p * 128 + to * 32 : p * 128 + to * 32 + 32, :]

            for m in (1, 2, 3):
                spread(chunk, m).start()
            keep(chunk).start()

    @pl.loop(0, NCH)
    def _(chunk):
        shift(chunk, z, up, 0).wait_send()
        shift(chunk, z, down, 1).wait_send()
        shift(chunk, far, up, 2).wait_send()
        keep(chunk).wait()
        for m in (1, 2, 3):
            spread(chunk, m).wait_send()
            src = lax.rem(q + m, 4)
            pltpu.make_async_remote_copy(
                src_ref=ob.at[src, :, pl.ds(chunk * CK, CK)],
                dst_ref=out.at[:, src, pl.ds(chunk * CK, CK)],
                send_sem=so.at[src, chunk], recv_sem=ro.at[src, chunk],
                device_id=(plane_tile(src, z), chan), device_id_type=MESH,
            ).wait_recv()


VM = pl.BlockSpec(memory_space=pltpu.VMEM)
ANY = pl.BlockSpec(memory_space=pl.ANY)
LIMIT = 60 << 20


def body(voltages, history, filter_taps):
    fine, coarse = (jnp.asarray(x) for x in phase_tables())
    got = pl.pallas_call(
        front_kernel,
        name="front",
        out_shape=jax.ShapeDtypeStruct((4, CHAN, 256, 128), BF16),
        in_specs=[VM, ANY, VM, VM, VM],
        out_specs=ANY,
        scratch_shapes=[
            pltpu.VMEM((8, (TAPS - 1) * FFT), jnp.int32),
            pltpu.VMEM((2 * CH, FFT), BF16),
            pltpu.VMEM((ROWS * SLOC, 128), F32),
            pltpu.VMEM((128, 128), F32),
            pltpu.VMEM((CHAN, NT, OWN * SLOC, 128), BF16),
            pltpu.VMEM((CHAN, NT, OWN * SLOC, 128), BF16),
            pltpu.VMEM((80 * 8, 128), F32),
            pltpu.VMEM((OWN * SPEC, FFT), BF16),
            pltpu.VMEM((OWN * SPEC, 128), F32),
            pltpu.VMEM((128 * 8, 128), F32),
            pltpu.VMEM((CHAN, 4, 256, 128), BF16),
            pltpu.SemaphoreType.DMA,
            pltpu.SemaphoreType.DMA((CHAN,)),
            pltpu.SemaphoreType.DMA((CHAN,)),
            pltpu.SemaphoreType.DMA((CHAN, 4)),
            pltpu.SemaphoreType.DMA((4, CHAN)),
            pltpu.SemaphoreType.DMA,
        ],
        compiler_params=pltpu.CompilerParams(
            collective_id=0, has_side_effects=True, vmem_limit_bytes=LIMIT
        ),
    )(voltages, history, filter_taps, fine, coarse)
    vis = pl.pallas_call(
        back_kernel,
        name="back",
        out_shape=jax.ShapeDtypeStruct((2, 4, KD, ROWS, INPUTS), BF16),
        in_specs=[VM],
        out_specs=ANY,
        scratch_shapes=[
            pltpu.VMEM((KD, 2, 4, 64, 256), BF16),
            pltpu.VMEM((4, 2, KD, ROWS, INPUTS), BF16),
            pltpu.SemaphoreType.DMA((3, NCH)),
            pltpu.SemaphoreType.DMA((3, NCH)),
            pltpu.SemaphoreType.DMA((4, NCH)),
            pltpu.SemaphoreType.DMA((4, NCH)),
            pltpu.SemaphoreType.DMA((NCH,)),
        ],
        compiler_params=pltpu.CompilerParams(
            collective_id=1, has_side_effects=True, vmem_limit_bytes=LIMIT
        ),
    )(got)
    return vis.reshape(2, 4 * KD, ROWS, INPUTS).astype(F32)


def solution(mesh):
    in_specs = (P("tile", "chan"), P("tile", None), P())
    out_specs = P(None, "chan", "tile", None)
    return jax.shard_map(body, mesh=mesh, in_specs=in_specs, out_specs=out_specs, check_vma=False)
```

time: 410 us -> 210 us (0.51)
  Pallas kernels: 0 us -> 197 us
  waiting for transfers between devices: 165 us -> 0 us
  local copies, waits for them, and re-layouts: 68.6 us -> 0 us
  matrix products: 65.5 us -> 0 us
  other arithmetic: 59.2 us -> 12 us
  blocking collectives: 31.9 us -> 0 us
  between operations: 13.5 us -> 0.02 us
  starting transfers between devices: 5.58 us -> 0 us
    pallas_call x0 -> x2, Pallas kernels: none -> 197 us  [the longest x1 124 us: body(): pl.pallas_call(back_kernel, name='back', out_shape=jax.ShapeDtypeStruct((...]
    all_gather x1 -> x0, waiting for transfers between devices: 165 us -> none  [body(): lax.all_gather(turned, 'tile', axis=0, tiled=True)]
    dot_general x2 -> x0, matrix products: 65.5 us -> none  [the longest x1 43.5 us: body(): jnp.dot(filtered.reshape(-1, FFT), dft_table(FFT, CH), preferred_element_...]
    another operation x3 -> x0, other arithmetic: 40.2 us -> none
    all_to_all x1 -> x0, blocking collectives: 31.9 us -> none  [body(): lax.all_to_all(spectra, 'chan', split_axis=3, concat_axis=1, tiled=True)]
    unnamed x10 -> x0, local copies, waits for them, and re-layouts: 19.5 us -> none
    all_to_all x2 -> x0, local copies, waits for them, and re-layouts: 13.2 us -> none  [body(): lax.all_to_all(spectra, 'chan', split_axis=3, concat_axis=1, tiled=True)]
    convert_element_type x1 -> x0, local copies, waits for them, and re-layouts: 12.8 us -> none  [body(): spectra.reshape(local_inputs, spectra_count, 2, CH).astype(jnp.bfloat16)]
  transfers between devices with their start and end apart: 2 -> 0, of which waited for: 1 -> 0; matrix products, arithmetic and copies ran while one was open for 13% -> 0% of each run, Pallas kernels for 0% -> 0%
where the time goes in v1:
time: 210 us; the launch traced here: 209 us
  Pallas kernels  197 us (94%)
  other arithmetic  12 us (6%)
    pallas_call x1, Pallas kernels, body(): pl.pallas_call(back_kernel, name='back', out_shape=jax.ShapeDtypeStruct((...  124 us
    pallas_call x1, Pallas kernels, body(): pl.pallas_call(front_kernel, name='front', out_shape=jax.ShapeDtypeStruct...  73.1 us
    convert_element_type x1, other arithmetic, body(): return vis.reshape(2, 4 * KD, ROWS, INPUTS).astype(F32)  12 us

profile of v1, /device:TPU:1, one launch (start us, length us, event | category | flops | bytes accessed | tf_op | source)
XLA Modules:
  0.0 209.5 jit_solution(6226287376087247762)
XLA Ops:
  0.0 73.1 %front.1.got = bf16[4,8,256,128]{3,2,1,0:T(8,128)(2,1)} custom-call(s32[32,32768]{1,0:T(8,128)} %volt.1, s32[32,30720]{1,0:T(8,128)} %hist.1, s32[16,2048]{1,0:T(8,128)} %taps.1, f32[2,1024,128]{2,1,0:T(8,128)} %constant.4.clone.fine, f32[2,16,16,128]{3,2,1,0:T(8,128)} %constant.5.clone.coarse), custom_call_target="tpu_custom_call" | custom-call | tf_op jit(solution)/shard_map/front/pallas_call | solution.py:344
  73.1 124.4 %back.1 = bf16[2,4,32,32,512]{4,3,2,1,0:T(8,128)(2,1)} custom-call(bf16[4,8,256,128]{3,2,1,0:T(8,128)(2,1)} %front.1.got), custom_call_target="tpu_custom_call" | custom-call | tf_op jit(solution)/shard_map/back/pallas_call | solution.py:373
  197.5 12.0 %convert.1 = f32[2,128,32,512]{3,2,1,0:T(8,128)} convert(bf16[2,128,32,512]{3,2,1,0:T(8,128)(2,1)} %bitcast.2) | non-fusion elementwise | flops 4194304 | bytes 25165824 | tf_op jit(solution)/shard_map/convert_element_type | solution.py:392

commit v2 on v1

v2 whole, which is shorter than its diff:
```python
import functools
import math

import jax
import jax.numpy as jnp
import numpy as np
from jax import lax
from jax.experimental import pallas as pl
from jax.experimental.pallas import tpu as pltpu
from jax.sharding import PartitionSpec as P

CH = 1024
TAPS = 16
FFT = 2048
SPEC = 128
INPUTS = 512

NT = FFT // 128
CHAN = 8
ROWS = 32
OWN = ROWS // CHAN
SLOC = SPEC // CHAN
RC = 4
NR = NT // RC
CHUNKS = 4
MIXED = 6
KEPT = 4
PER = MIXED + KEPT
GROUP = 4 * MIXED + 2 * KEPT
STEP = 2
SUBS = PER // STEP
NSUB = CHUNKS * SUBS
AHEAD = 2
LIMIT = 62 << 20
DBG = ()

MESH = pl.DeviceIdType.MESH
F32 = jnp.float32
BF16 = jnp.bfloat16


def phase_tables():
    k = np.arange(CH, dtype=np.int64).reshape(CHAN, CHUNKS, GROUP).transpose(1, 0, 2).reshape(-1)
    fine = (k[:, None] * np.arange(128)[None, :]) % FFT * (2.0 * math.pi / FFT)
    fine = np.stack([np.cos(fine), np.sin(fine)]) / math.sqrt(CH)
    coarse = (np.arange(NT)[:, None] * np.arange(16)[None, :]) % 16 * (2.0 * math.pi / 16)
    coarse = np.stack([np.cos(coarse), np.sin(coarse)])
    coarse = np.broadcast_to(coarse[..., None], (2, NT, 16, 128))
    return fine.astype(np.float32), np.ascontiguousarray(coarse).astype(np.float32)


def place():
    tile, chan = lax.axis_index("tile"), lax.axis_index("chan")
    x_lo, z, core = tile // 8, (tile // 2) % 4, tile % 2
    return tile, chan, x_lo, z, core


def plane_tile(q, z):
    return (q // 2) * 8 + z * 2 + q % 2


def kernel(
    volt, hist, taps, fine, coarse, out,
    h8, table, pack, hpack, send, recv, ext, filt, fir, spec, out2, got, gather, obm, obk,
    hsem, s1, r1, s2, r2, sz, rz, sm, rm, sk, rk, lsem,
):
    tile, chan, x_lo, z, core = place()
    q = x_lo * 2 + core
    up, down, far = lax.rem(z + 1, 4), lax.rem(z + 3, 4), lax.rem(z + 2, 4)
    hcopy = pltpu.make_async_copy(
        hist.at[pl.ds(pl.multiple_of((chan // 2) * 8, 8), 8), :], h8, hsem
    )
    hcopy.start()

    barrier = pltpu.get_barrier_semaphore()

    @pl.loop(1, 32)
    def _(i):
        other = lax.rem(q * 8 + chan + i, 32)
        pl.semaphore_signal(
            barrier, inc=1, device_id=(plane_tile(other // 8, z), other % 8), device_id_type=MESH
        )

    for nz in (up, down):
        pl.semaphore_signal(
            barrier, inc=1, device_id=(plane_tile(q, nz), chan), device_id_type=MESH
        )

    def first(i, r):
        to = lax.rem(chan + i, CHAN)
        part = pl.ds(r * NR, NR)
        return pltpu.make_async_remote_copy(
            src_ref=send.at[to, part], dst_ref=recv.at[chan, part],
            send_sem=s1.at[r, to], recv_sem=r1.at[r, chan],
            device_id=(tile, to), device_id_type=MESH,
        )

    def first_in(i, r):
        src = lax.rem(chan + CHAN - i, CHAN)
        part = pl.ds(r * NR, NR)
        return pltpu.make_async_remote_copy(
            src_ref=send.at[src, part], dst_ref=recv.at[src, part],
            send_sem=s1.at[r, src], recv_sem=r1.at[r, src],
            device_id=(tile, src), device_id_type=MESH,
        )

    def pack_part(r):
        @pl.loop(r * NR, r * NR + NR)
        def _(nt):
            for s in range(SLOC):
                lanes = pl.ds(pl.multiple_of(s * FFT + nt * 128, 128), 128)
                pack[pl.ds(s, ROWS, stride=SLOC), :] = volt[:, lanes].astype(F32)
            for c in range(CHAN):
                send[c, nt] = pack[pl.ds(c * OWN * SLOC, OWN * SLOC), :].astype(BF16)

    def send_part(r):
        @pl.loop(1, CHAN)
        def _(i):
            first(i, r).start()

    pack_part(0)
    pl.semaphore_wait(barrier, 33)
    send_part(0)

    @pl.loop(1, RC)
    def _(r):
        pack_part(r)
        send_part(r)

    recv[chan] = send[chan]
    hcopy.wait()

    @pl.loop(0, CH // 16)
    def _(kb):
        rows = pl.ds(pl.multiple_of(kb * 16, 16), 16)
        chunk = kb // 16
        base = chunk * 512 + lax.rem(kb, 16) * 16
        rows_re = pl.ds(pl.multiple_of(base, 16), 16)
        rows_im = pl.ds(pl.multiple_of(base + 256, 16), 16)
        c2, s2_ = fine[0, rows, :], fine[1, rows, :]
        for n1 in range(NT):
            c1, s1_ = coarse[0, n1], coarse[1, n1]
            lanes = pl.ds(n1 * 128, 128)
            table[rows_re, lanes] = (c1 * c2 - s1_ * s2_).astype(BF16)
            table[rows_im, lanes] = (-(s1_ * c2 + c1 * s2_)).astype(BF16)

    odd = lax.rem(chan, 2)

    @pl.loop(0, NT)
    def _(nt):
        @pl.when(lax.rem(nt, NR) == 0)
        def _():
            @pl.loop(1, CHAN)
            def _(i):
                first_in(i, nt // NR).wait_recv()

        for j in range(TAPS - 1):
            lanes = pl.ds(pl.multiple_of(j * FFT + nt * 128, 128), 128)
            hpack[pl.ds(j + 1, 8, stride=16), :] = h8[:, lanes].astype(F32)
        for a in range(OWN):
            old = hpack[pl.ds(pl.multiple_of(odd * 64 + a * 16, 16), 16), :]
            ext[pl.ds(a * 2, 16, stride=8), :] = old
        for c in range(CHAN):
            for a in range(OWN):
                part = recv[c, nt, a * 16 : (a + 1) * 16, :].astype(F32)
                start = (16 + (c % 4) * 16) * 8 + a * 2 + c // 4
                ext[pl.ds(start, 16, stride=8), :] = part
                if c == 3:
                    ext[pl.ds(a * 2 + 1, 16, stride=8), :] = part
        lanes = pl.ds(pl.multiple_of(nt * 128, 128), 128)
        weights = [
            jnp.broadcast_to(taps[t : t + 1, lanes].astype(F32), (8, 128)) for t in range(TAPS)
        ]

        @pl.loop(0, 64, step=8)
        def _(j0):
            base = pl.multiple_of(j0 * 8, 64)
            rows = [ext[pl.ds(base + (r + 1) * 8, 8), :] for r in range(8 + TAPS - 1)]
            for j in range(8):
                total = weights[0] * rows[j]
                for t in range(1, TAPS):
                    total = total + weights[t] * rows[j + t]
                fir[pl.ds(j0 + j, 8, stride=64), :] = total * (1.0 / 16384.0)

        filt[:, lanes] = fir[...].astype(BF16)

    def second(chunk, to, to_chan, src, src_chan):
        return pltpu.make_async_remote_copy(
            src_ref=out2.at[chunk, to_chan, to], dst_ref=got.at[chunk, src, src_chan],
            send_sem=s2.at[chunk, to, to_chan], recv_sem=r2.at[chunk, src, src_chan],
            device_id=(plane_tile(to, z), to_chan), device_id_type=MESH,
        )

    def dft(chunk):
        for p in range(2):
            rows = pl.ds(pl.multiple_of(chunk * 512 + p * 256, 256), 256)
            block = lax.dot_general(
                table[rows, :], filt[...], (((1,), (1,)), ((), ())), preferred_element_type=F32
            )
            for a in range(OWN):
                spec[pl.ds(p * OWN + a, 256, stride=8), :] = block[:, a * 128 : (a + 1) * 128]
        for c in range(CHAN):
            for to in range(4):
                start = (c * GROUP + MIXED * to) * 8
                out2[chunk, c, to, 0 : MIXED * 8, :] = spec[start : start + MIXED * 8, :].astype(BF16)
                start = (c * GROUP + 4 * MIXED + KEPT * (to % 2)) * 8
                out2[chunk, c, to, MIXED * 8 : PER * 8, :] = spec[start : start + KEPT * 8, :].astype(BF16)
        got[chunk, q, chan] = out2[chunk, chan, q]

        @pl.loop(1, 32)
        def _(i):
            other = lax.rem(q * 8 + chan + i, 32)
            second(chunk, other // 8, other % 8, q, chan).start()

    def arrive(chunk):
        @pl.loop(1, 32)
        def _(i):
            other = lax.rem(q * 8 + chan + 32 - i, 32)
            second(chunk, other // 8, other % 8, other // 8, other % 8).wait_recv()

    low = lax.broadcasted_iota(jnp.int32, (8, 128), 0) < 4

    def assemble(chunk):
        @pl.loop(0, PER // 2)
        def _(kp):
            rows = pl.ds(pl.multiple_of(kp * 16, 16), 16)
            for member in range(4):
                mx, mc = member // 2, member % 2
                for half in range(2):
                    parts = [
                        got[chunk, member, half * 4 + c, rows, :].astype(F32) for c in range(4)
                    ]
                    for kk in range(2):
                        v = [part[kk * 8 : kk * 8 + 8, :] for part in parts]
                        r = [pltpu.roll(x, 4, 0) for x in v]
                        re = jnp.concatenate(
                            [jnp.where(low, v[0], r[1]), jnp.where(low, v[2], r[3])], axis=0
                        )
                        im = jnp.concatenate(
                            [jnp.where(low, r[0], v[1]), jnp.where(low, r[2], v[3])], axis=0
                        )
                        at = pl.ds(mc * 32 + half * 16, 16)
                        channel = chunk * PER + kp * 2 + kk
                        gather[channel, mx, z, at, 0:128] = re.astype(BF16)
                        gather[channel, mx, z, at, 128:256] = im.astype(BF16)

    def split(step):
        return step // SUBS, lax.rem(step, SUBS)

    def channel_of(step):
        chunk, j = split(step)
        return chunk * PER + jnp.where(lax.rem(j, 2) == 0, j, MIXED - 1 + j)

    def shift(step, owner, to, way):
        block = gather.at[pl.ds(channel_of(step), STEP), :, owner]
        return pltpu.make_async_remote_copy(
            src_ref=block, dst_ref=block, send_sem=sz.at[way, step], recv_sem=rz.at[way, step],
            device_id=(plane_tile(q, to), chan), device_id_type=MESH,
        )

    def mixed_rows(chunk, j, src):
        return out.at[:, pl.ds(chunk * GROUP + MIXED * src + j, STEP)]

    def mixed_part(chunk, j, to):
        return obm.at[to, :, pl.ds(chunk * MIXED + j, STEP)]

    def spread(chunk, j, to, src):
        at = chunk * (MIXED // 2) + j // 2
        return pltpu.make_async_remote_copy(
            src_ref=mixed_part(chunk, j, to), dst_ref=mixed_rows(chunk, j, src),
            send_sem=sm.at[to, at], recv_sem=rm.at[src, at],
            device_id=(plane_tile(to, z), chan), device_id_type=MESH,
        )

    def spread_own(chunk, j):
        return pltpu.make_async_copy(
            mixed_part(chunk, j, q), mixed_rows(chunk, j, q), lsem.at[chunk * SUBS + j]
        )

    def kept_rows(chunk, j, src):
        return out.at[:, pl.ds(chunk * GROUP + 4 * MIXED + KEPT * src + j - 1, STEP)]

    def kept_part(chunk, j, to):
        return obk.at[to, :, pl.ds(chunk * KEPT + j - 1, STEP)]

    def pair(chunk, j, src):
        at = chunk * (KEPT // 2) + j // 2
        return pltpu.make_async_remote_copy(
            src_ref=kept_part(chunk, j, 1 - core), dst_ref=kept_rows(chunk, j, src),
            send_sem=sk.at[at], recv_sem=rk.at[at],
            device_id=(plane_tile(x_lo * 2 + 1 - core, z), chan), device_id_type=MESH,
        )

    def pair_own(chunk, j):
        return pltpu.make_async_copy(
            kept_part(chunk, j, core), kept_rows(chunk, j, core), lsem.at[chunk * SUBS + j]
        )

    def correlate(mine, right):
        re, im = mine[:, :128], mine[:, 128:]
        left = jnp.concatenate([mine, jnp.concatenate([im, -re], axis=1)], axis=0)
        vis = lax.dot_general(left, right, (((1,), (1,)), ((), ())), preferred_element_type=F32)
        return (vis * (1.0 / SPEC)).astype(BF16)

    @pl.loop(0, 2)
    def _(chunk):
        dft(chunk)

    @pl.loop(0, NSUB + AHEAD + 1)
    def _(tick):
        @pl.when(tick < NSUB)
        def _():
            chunk, j = split(tick)

            @pl.when(j == 0)
            def _():
                arrive(chunk)
                assemble(chunk)

            shift(tick, z, up, 0).start()
            shift(tick, z, down, 1).start()

        @pl.when(tick < CHUNKS - 2)
        def _():
            dft(tick + 2)

        step = tick - AHEAD

        @pl.when((step >= 0) & (step < NSUB))
        def _():
            shift(step, down, up, 0).wait_recv()
            shift(step, up, down, 1).wait_recv()

            @pl.when(lax.rem(step, 2) == 0)
            def _():
                shift(step, down, up, 2).start()

            @pl.when(lax.rem(step, 2) == 1)
            def _():
                shift(step, up, down, 2).start()

        @pl.when(step > 0)
        def _():
            done = step - 1
            shift(done, far, up, 2).wait_recv()
            chunk, j = split(done)
            base = channel_of(done)

            @pl.when(lax.rem(j, 2) == 0)
            def _():
                for kk in range(STEP):
                    mine = gather[base + kk, :, z].reshape(128, 256)
                    vis = correlate(mine, gather[base + kk].reshape(INPUTS, 256))
                    for to in range(4):
                        for p in range(2):
                            first_row = p * 128 + to * 32
                            obm[to, p, chunk * MIXED + j + kk] = vis[first_row : first_row + 32, :]
                for m in (1, 2, 3):
                    spread(chunk, j, lax.rem(q + m, 4), q).start()
                spread_own(chunk, j).start()

            @pl.when(lax.rem(j, 2) == 1)
            def _():
                for kk in range(STEP):
                    mine = gather[base + kk, x_lo, z]
                    vis = correlate(mine, gather[base + kk].reshape(INPUTS, 256))
                    for to in range(2):
                        for p in range(2):
                            first_row = p * 64 + to * 32
                            obk[to, p, chunk * KEPT + j - 1 + kk] = vis[first_row : first_row + 32, :]
                pair(chunk, j, core).start()
                pair_own(chunk, j).start()

    @pl.loop(0, RC)
    def _(r):
        @pl.loop(1, CHAN)
        def _(i):
            first(i, r).wait_send()

    @pl.loop(0, CHUNKS)
    def _(chunk):
        @pl.loop(1, 32)
        def _(i):
            other = lax.rem(q * 8 + chan + i, 32)
            second(chunk, other // 8, other % 8, q, chan).wait_send()

    @pl.loop(0, NSUB)
    def _(step):
        shift(step, z, up, 0).wait_send()
        shift(step, z, down, 1).wait_send()
        shift(step, far, up, 2).wait_send()
        chunk, j = split(step)

        @pl.when(lax.rem(j, 2) == 0)
        def _():
            spread_own(chunk, j).wait()
            for m in (1, 2, 3):
                other = lax.rem(q + m, 4)
                spread(chunk, j, other, q).wait_send()
                spread(chunk, j, other, other).wait_recv()

        @pl.when(lax.rem(j, 2) == 1)
        def _():
            pair_own(chunk, j).wait()
            pair(chunk, j, core).wait_send()
            pair(chunk, j, 1 - core).wait_recv()


VM = pl.BlockSpec(memory_space=pltpu.VMEM)
ANY = pl.BlockSpec(memory_space=pl.ANY)
DMA = pltpu.SemaphoreType.DMA


def body(voltages, history, filter_taps):
    fine, coarse = (jnp.asarray(x) for x in phase_tables())
    vis = pl.pallas_call(
        kernel,
        name="correlator",
        out_shape=jax.ShapeDtypeStruct((2, CHUNKS * GROUP, ROWS, INPUTS), BF16),
        in_specs=[VM, ANY, VM, VM, VM],
        out_specs=ANY,
        scratch_shapes=[
            pltpu.VMEM((8, (TAPS - 1) * FFT), jnp.int32),
            pltpu.VMEM((2 * CH, FFT), BF16),
            pltpu.VMEM((ROWS * SLOC, 128), F32),
            pltpu.VMEM((128, 128), F32),
            pltpu.VMEM((CHAN, NT, OWN * SLOC, 128), BF16),
            pltpu.VMEM((CHAN, NT, OWN * SLOC, 128), BF16),
            pltpu.VMEM((80 * 8, 128), F32),
            pltpu.VMEM((OWN * SPEC, FFT), BF16),
            pltpu.VMEM((OWN * SPEC, 128), F32),
            pltpu.VMEM((256 * 8, 128), F32),
            pltpu.VMEM((CHUNKS, CHAN, 4, PER * 8, 128), BF16),
            pltpu.VMEM((CHUNKS, 4, CHAN, PER * 8, 128), BF16),
            pltpu.VMEM((CHUNKS * PER, 2, 4, 64, 256), BF16),
            pltpu.VMEM((4, 2, CHUNKS * MIXED, ROWS, INPUTS), BF16),
            pltpu.VMEM((2, 2, CHUNKS * KEPT, ROWS, INPUTS), BF16),
            DMA,
            DMA((RC, CHAN)),
            DMA((RC, CHAN)),
            DMA((CHUNKS, 4, CHAN)),
            DMA((CHUNKS, 4, CHAN)),
            DMA((3, NSUB)),
            DMA((3, NSUB)),
            DMA((4, CHUNKS * MIXED // 2)),
            DMA((4, CHUNKS * MIXED // 2)),
            DMA((CHUNKS * KEPT // 2,)),
            DMA((CHUNKS * KEPT // 2,)),
            DMA((NSUB,)),
        ],
        compiler_params=pltpu.CompilerParams(
            collective_id=0, has_side_effects=True, vmem_limit_bytes=LIMIT
        ),
    )(voltages, history, filter_taps, fine, coarse)
    return vis.astype(F32)


def solution(mesh):
    in_specs = (P("tile", "chan"), P("tile", None), P())
    out_specs = P(None, "chan", "tile", None)
    return jax.shard_map(body, mesh=mesh, in_specs=in_specs, out_specs=out_specs, check_vma=False)
```

time: 210 us -> 165 us (0.79)
  Pallas kernels: 197 us -> 152 us
    pallas_call x2 -> x1, Pallas kernels: 197 us -> 152 us  [body(): pl.pallas_call(kernel, name='correlator', out_shape=jax.ShapeDtypeStruct(...]
where the time goes in v2:
time: 165 us; the launch traced here: 164 us
  Pallas kernels  152 us (92%)
  other arithmetic  12 us (7%)
    pallas_call x1, Pallas kernels, body(): pl.pallas_call(kernel, name='correlator', out_shape=jax.ShapeDtypeStruct(...  152 us
    convert_element_type x1, other arithmetic, body(): return vis.astype(F32)  12 us

profile of v2, /device:TPU:1, one launch (start us, length us, event | category | flops | bytes accessed | tf_op | source)
XLA Modules:
  0.0 163.6 jit_solution(2823104003415678925)
XLA Ops:
  0.0 151.7 %correlator.1 = bf16[2,128,32,512]{3,2,1,0:T(8,128)(2,1)} custom-call(s32[32,32768]{1,0:T(8,128)} %volt.1, s32[32,30720]{1,0:T(8,128)} %hist.1, s32[16,2048]{1,0:T(8,128)} %taps.1, f32[2,1024,128]{2,1,0:T(8,128)} %constant.4.clone.fine, f32[2,16,16,128]{3,2,1,0:T(8,128)} %constant.5.clone.coarse), custom_call_target="tpu_custom_call" | custom-call | tf_op jit(solution)/shard_map/correlator/pallas_call | solution.py:416
  151.7 12.0 %convert_element_type.3 = f32[2,128,32,512]{3,2,1,0:T(8,128)} convert(bf16[2,128,32,512]{3,2,1,0:T(8,128)(2,1)} %correlator.1) | non-fusion elementwise | flops 4194304 | bytes 25165824 | tf_op jit(solution)/shard_map/convert_element_type | solution.py:455

commit v3 on v2

--- a/solution.py
+++ b/solution.py
@@ -30,9 +30,12 @@
 STEP = 2
 SUBS = PER // STEP
 NSUB = CHUNKS * SUBS
-AHEAD = 2
-LIMIT = 62 << 20
-DBG = ()
+EARLY = 3
+AHEAD = 1
+LAG = 1
+LIMIT = 54 << 20
+WIDE = 4
+SLOTS = 8
 
 MESH = pl.DeviceIdType.MESH
 F32 = jnp.float32
@@ -60,17 +63,28 @@
 
 
 def kernel(
-    volt, hist, taps, fine, coarse, out,
-    h8, table, pack, hpack, send, recv, ext, filt, fir, spec, out2, got, gather, obm, obk,
-    hsem, s1, r1, s2, r2, sz, rz, sm, rm, sk, rk, lsem,
+    volts, hist, taps, fines, coarses, out,
+    volt, h8, fine, coarse, table, pack, hpack, send, recv, ext, filt, fir, spec, out2, got, gather, obm, obk,
+    vsem, hsem, s1, r1, s2, r2, sz, rz, sm, rm, sk, rk, lsem,
 ):
     tile, chan, x_lo, z, core = place()
     q = x_lo * 2 + core
     up, down, far = lax.rem(z + 1, 4), lax.rem(z + 3, 4), lax.rem(z + 2, 4)
-    hcopy = pltpu.make_async_copy(
-        hist.at[pl.ds(pl.multiple_of((chan // 2) * 8, 8), 8), :], h8, hsem
-    )
-    hcopy.start()
+    samples = [
+        pltpu.make_async_copy(volts.at[:, pl.ds(s * FFT, FFT)], volt.at[s], vsem.at[s])
+        for s in range(SLOC)
+    ]
+    for copy in samples:
+        copy.start()
+    later = [
+        pltpu.make_async_copy(
+            hist.at[pl.ds(pl.multiple_of((chan // 2) * 8, 8), 8), :], h8, hsem.at[0]
+        ),
+        pltpu.make_async_copy(fines, fine, hsem.at[1]),
+        pltpu.make_async_copy(coarses, coarse, hsem.at[2]),
+    ]
+    for copy in later:
+        copy.start()
 
     barrier = pltpu.get_barrier_semaphore()
 
@@ -108,8 +122,8 @@
         @pl.loop(r * NR, r * NR + NR)
         def _(nt):
             for s in range(SLOC):
-                lanes = pl.ds(pl.multiple_of(s * FFT + nt * 128, 128), 128)
-                pack[pl.ds(s, ROWS, stride=SLOC), :] = volt[:, lanes].astype(F32)
+                lanes = pl.ds(pl.multiple_of(nt * 128, 128), 128)
+                pack[pl.ds(s, ROWS, stride=SLOC), :] = volt[s, :, lanes].astype(F32)
             for c in range(CHAN):
                 send[c, nt] = pack[pl.ds(c * OWN * SLOC, OWN * SLOC), :].astype(BF16)
 
@@ -118,6 +132,8 @@
         def _(i):
             first(i, r).start()
 
+    for copy in samples:
+        copy.wait()
     pack_part(0)
     pl.semaphore_wait(barrier, 33)
     send_part(0)
@@ -128,7 +144,8 @@
         send_part(r)
 
     recv[chan] = send[chan]
-    hcopy.wait()
+    for copy in later:
+        copy.wait()
 
     @pl.loop(0, CH // 16)
     def _(kb):
@@ -244,28 +261,38 @@
                         gather[channel, mx, z, at, 0:128] = re.astype(BF16)
                         gather[channel, mx, z, at, 128:256] = im.astype(BF16)
 
+    def is_kept(j):
+        return (j == 1) | (j == 4)
+
+    def mixed_at(j):
+        return STEP * jnp.maximum(j - 1, 0)
+
+    def kept_at(j):
+        return 2 * (j // 4)
+
     def split(step):
         return step // SUBS, lax.rem(step, SUBS)
 
     def channel_of(step):
         chunk, j = split(step)
-        return chunk * PER + jnp.where(lax.rem(j, 2) == 0, j, MIXED - 1 + j)
+        return chunk * PER + jnp.where(is_kept(j), MIXED + kept_at(j), mixed_at(j))
 
     def shift(step, owner, to, way):
-        block = gather.at[pl.ds(channel_of(step), STEP), :, owner]
+        first_one = channel_of(step) + (STEP // 2 if way == 3 else 0)
+        block = gather.at[pl.ds(first_one, STEP if way < 2 else STEP // 2), :, owner]
         return pltpu.make_async_remote_copy(
             src_ref=block, dst_ref=block, send_sem=sz.at[way, step], recv_sem=rz.at[way, step],
             device_id=(plane_tile(q, to), chan), device_id_type=MESH,
         )
 
     def mixed_rows(chunk, j, src):
-        return out.at[:, pl.ds(chunk * GROUP + MIXED * src + j, STEP)]
+        return out.at[:, pl.ds(chunk * GROUP + MIXED * src + mixed_at(j), STEP)]
 
     def mixed_part(chunk, j, to):
-        return obm.at[to, :, pl.ds(chunk * MIXED + j, STEP)]
+        return obm.at[to, :, pl.ds(chunk * MIXED + mixed_at(j), STEP)]
 
     def spread(chunk, j, to, src):
-        at = chunk * (MIXED // 2) + j // 2
+        at = chunk * (MIXED // STEP) + mixed_at(j) // STEP
         return pltpu.make_async_remote_copy(
             src_ref=mixed_part(chunk, j, to), dst_ref=mixed_rows(chunk, j, src),
             send_sem=sm.at[to, at], recv_sem=rm.at[src, at],
@@ -278,13 +305,13 @@
         )
 
     def kept_rows(chunk, j, src):
-        return out.at[:, pl.ds(chunk * GROUP + 4 * MIXED + KEPT * src + j - 1, STEP)]
+        return out.at[:, pl.ds(chunk * GROUP + 4 * MIXED + KEPT * src + kept_at(j), STEP)]
 
     def kept_part(chunk, j, to):
-        return obk.at[to, :, pl.ds(chunk * KEPT + j - 1, STEP)]
+        return obk.at[to, :, pl.ds(chunk * KEPT + kept_at(j), STEP)]
 
     def pair(chunk, j, src):
-        at = chunk * (KEPT // 2) + j // 2
+        at = chunk * (KEPT // STEP) + kept_at(j) // STEP
         return pltpu.make_async_remote_copy(
             src_ref=kept_part(chunk, j, 1 - core), dst_ref=kept_rows(chunk, j, src),
             send_sem=sk.at[at], recv_sem=rk.at[at],
@@ -302,11 +329,11 @@
         vis = lax.dot_general(left, right, (((1,), (1,)), ((), ())), preferred_element_type=F32)
         return (vis * (1.0 / SPEC)).astype(BF16)
 
-    @pl.loop(0, 2)
+    @pl.loop(0, EARLY)
     def _(chunk):
         dft(chunk)
 
-    @pl.loop(0, NSUB + AHEAD + 1)
+    @pl.loop(0, NSUB + AHEAD + LAG)
     def _(tick):
         @pl.when(tick < NSUB)
         def _():
@@ -320,9 +347,9 @@
             shift(tick, z, up, 0).start()
             shift(tick, z, down, 1).start()
 
-        @pl.when(tick < CHUNKS - 2)
-        def _():
-            dft(tick + 2)
+        @pl.when(tick < CHUNKS - EARLY)
+        def _():
+            dft(tick + EARLY)
 
         step = tick - AHEAD
 
@@ -331,22 +358,18 @@
             shift(step, down, up, 0).wait_recv()
             shift(step, up, down, 1).wait_recv()
 
-            @pl.when(lax.rem(step, 2) == 0)
-            def _():
-                shift(step, down, up, 2).start()
-
-            @pl.when(lax.rem(step, 2) == 1)
-            def _():
-                shift(step, up, down, 2).start()
-
-        @pl.when(step > 0)
-        def _():
-            done = step - 1
+            shift(step, down, up, 2).start()
+            shift(step, up, down, 3).start()
+
+        @pl.when(step >= LAG)
+        def _():
+            done = step - LAG
             shift(done, far, up, 2).wait_recv()
+            shift(done, far, down, 3).wait_recv()
             chunk, j = split(done)
             base = channel_of(done)
 
-            @pl.when(lax.rem(j, 2) == 0)
+            @pl.when(jnp.logical_not(is_kept(j)))
             def _():
                 for kk in range(STEP):
                     mine = gather[base + kk, :, z].reshape(128, 256)
@@ -354,12 +377,12 @@
                     for to in range(4):
                         for p in range(2):
                             first_row = p * 128 + to * 32
-                            obm[to, p, chunk * MIXED + j + kk] = vis[first_row : first_row + 32, :]
+                            obm[to, p, chunk * MIXED + mixed_at(j) + kk] = vis[first_row : first_row + 32, :]
                 for m in (1, 2, 3):
                     spread(chunk, j, lax.rem(q + m, 4), q).start()
                 spread_own(chunk, j).start()
 
-            @pl.when(lax.rem(j, 2) == 1)
+            @pl.when(is_kept(j))
             def _():
                 for kk in range(STEP):
                     mine = gather[base + kk, x_lo, z]
@@ -367,7 +390,7 @@
                     for to in range(2):
                         for p in range(2):
                             first_row = p * 64 + to * 32
-                            obk[to, p, chunk * KEPT + j - 1 + kk] = vis[first_row : first_row + 32, :]
+                            obk[to, p, chunk * KEPT + kept_at(j) + kk] = vis[first_row : first_row + 32, :]
                 pair(chunk, j, core).start()
                 pair_own(chunk, j).start()
 
@@ -388,10 +411,11 @@
     def _(step):
         shift(step, z, up, 0).wait_send()
         shift(step, z, down, 1).wait_send()
-        shift(step, far, up, 2).wait_send()
+        shift(step, down, up, 2).wait_send()
+        shift(step, up, down, 3).wait_send()
         chunk, j = split(step)
 
-        @pl.when(lax.rem(j, 2) == 0)
+        @pl.when(jnp.logical_not(is_kept(j)))
         def _():
             spread_own(chunk, j).wait()
             for m in (1, 2, 3):
@@ -399,11 +423,37 @@
                 spread(chunk, j, other, q).wait_send()
                 spread(chunk, j, other, other).wait_recv()
 
-        @pl.when(lax.rem(j, 2) == 1)
+        @pl.when(is_kept(j))
         def _():
             pair_own(chunk, j).wait()
             pair(chunk, j, core).wait_send()
             pair(chunk, j, 1 - core).wait_recv()
+
+
+def widen(vis, out, wide, sem):
+    per_part = CHUNKS * GROUP // WIDE
+
+    def store(block):
+        slot = lax.rem(block, SLOTS)
+        return pltpu.make_async_copy(
+            wide.at[slot],
+            out.at[block // per_part, pl.ds(lax.rem(block, per_part) * WIDE, WIDE)],
+            sem.at[slot],
+        )
+
+    @pl.loop(0, 2 * per_part)
+    def _(block):
+        @pl.when(block >= SLOTS)
+        def _():
+            store(block - SLOTS).wait()
+
+        rows = pl.ds(lax.rem(block, per_part) * WIDE, WIDE)
+        wide[lax.rem(block, SLOTS)] = vis[block // per_part, rows].astype(F32)
+        store(block).start()
+
+    @pl.loop(2 * per_part - SLOTS, 2 * per_part)
+    def _(block):
+        store(block).wait()
 
 
 VM = pl.BlockSpec(memory_space=pltpu.VMEM)
@@ -416,11 +466,14 @@
     vis = pl.pallas_call(
         kernel,
         name="correlator",
-        out_shape=jax.ShapeDtypeStruct((2, CHUNKS * GROUP, ROWS, INPUTS), BF16),
-        in_specs=[VM, ANY, VM, VM, VM],
-        out_specs=ANY,
+        out_shape=pltpu.VMEM((2, CHUNKS * GROUP, ROWS, INPUTS), BF16),
+        in_specs=[ANY, ANY, VM, ANY, ANY],
+        out_specs=VM,
         scratch_shapes=[
+            pltpu.VMEM((SLOC, ROWS, FFT), jnp.int32),
             pltpu.VMEM((8, (TAPS - 1) * FFT), jnp.int32),
+            pltpu.VMEM((2, CH, 128), F32),
+            pltpu.VMEM((2, NT, 16, 128), F32),
             pltpu.VMEM((2 * CH, FFT), BF16),
             pltpu.VMEM((ROWS * SLOC, 128), F32),
             pltpu.VMEM((128, 128), F32),
@@ -435,13 +488,14 @@
             pltpu.VMEM((CHUNKS * PER, 2, 4, 64, 256), BF16),
             pltpu.VMEM((4, 2, CHUNKS * MIXED, ROWS, INPUTS), BF16),
             pltpu.VMEM((2, 2, CHUNKS * KEPT, ROWS, INPUTS), BF16),
-            DMA,
+            DMA((SLOC,)),
+            DMA((3,)),
             DMA((RC, CHAN)),
             DMA((RC, CHAN)),
             DMA((CHUNKS, 4, CHAN)),
             DMA((CHUNKS, 4, CHAN)),
-            DMA((3, NSUB)),
-            DMA((3, NSUB)),
+            DMA((4, NSUB)),
+            DMA((4, NSUB)),
             DMA((4, CHUNKS * MIXED // 2)),
             DMA((4, CHUNKS * MIXED // 2)),
             DMA((CHUNKS * KEPT // 2,)),
@@ -452,7 +506,15 @@
             collective_id=0, has_side_effects=True, vmem_limit_bytes=LIMIT
         ),
     )(voltages, history, filter_taps, fine, coarse)
-    return vis.astype(F32)
+    return pl.pallas_call(
+        widen,
+        name="widen",
+        out_shape=jax.ShapeDtypeStruct((2, CHUNKS * GROUP, ROWS, INPUTS), F32),
+        in_specs=[VM],
+        out_specs=ANY,
+        scratch_shapes=[pltpu.VMEM((SLOTS, WIDE, ROWS, INPUTS), F32), DMA((SLOTS,))],
+        compiler_params=pltpu.CompilerParams(vmem_limit_bytes=32 << 20),
+    )(vis)
 
 
 def solution(mesh):

time: 165 us -> 155 us (0.939)
  other arithmetic: 12 us -> 0 us
  Pallas kernels: 152 us -> 155 us
    convert_element_type x1 -> x0, other arithmetic: 12 us -> none  [body(): return vis.astype(F32)]
    pallas_call x1 -> x2, Pallas kernels: 152 us -> 155 us  [the longest x1 149 us: body(): pl.pallas_call(kernel, name='correlator', out_shape=pltpu.VMEM((2, CHUNKS...]
where the time goes in v3:
time: 155 us
  Pallas kernels  155 us (100%)
    pallas_call x1, Pallas kernels, body(): pl.pallas_call(kernel, name='correlator', out_shape=pltpu.VMEM((2, CHUNKS...  149 us
    pallas_call x1, Pallas kernels, body(): pl.pallas_call(widen, name='widen', out_shape=jax.ShapeDtypeStruct((2, CH...  6.44 us

profile of v3, /device:TPU:1, one launch (start us, length us, event | category | flops | bytes accessed | tf_op | source)
XLA Modules:
  0.0 155.0 jit_solution(2206253713742177971)
XLA Ops:
  0.0 148.5 %correlator.1.vis = bf16[2,128,32,512]{3,2,1,0:T(8,128)(2,1)S(1)} custom-call(s32[32,32768]{1,0:T(8,128)} %volts.1, s32[32,30720]{1,0:T(8,128)} %hist.1, s32[16,2048]{1,0:T(8,128)} %taps.1, f32[2,1024,128]{2,1,0:T(8,128)} %constant.4.clone.fines, f32[2,16,16,128]{3,2,1,0:T(8,128)} %constant.5.clone.coarses), custom_call_target="tpu_custom_call" | custom-call | tf_op jit(solution)/shard_map/correlator/pallas_call | solution.py:466
  148.5 6.4 %widen.1 = f32[2,128,32,512]{3,2,1,0:T(8,128)} custom-call(bf16[2,128,32,512]{3,2,1,0:T(8,128)(2,1)S(1)} %correlator.1.vis), custom_call_target="tpu_custom_call" | custom-call | tf_op jit(solution)/shard_map/widen/pallas_call | solution.py:509

commit v4 on v3

--- a/solution.py
+++ b/solution.py
@@ -20,7 +20,7 @@
 ROWS = 32
 OWN = ROWS // CHAN
 SLOC = SPEC // CHAN
-RC = 4
+RC = 8
 NR = NT // RC
 CHUNKS = 4
 MIXED = 6
@@ -30,7 +30,8 @@
 STEP = 2
 SUBS = PER // STEP
 NSUB = CHUNKS * SUBS
-EARLY = 3
+EARLY = 1
+GAP = 3
 AHEAD = 1
 LAG = 1
 LIMIT = 54 << 20
@@ -347,9 +348,9 @@
             shift(tick, z, up, 0).start()
             shift(tick, z, down, 1).start()
 
-        @pl.when(tick < CHUNKS - EARLY)
-        def _():
-            dft(tick + EARLY)
+        @pl.when((lax.rem(tick, GAP) == 0) & (tick // GAP < CHUNKS - EARLY))
+        def _():
+            dft(tick // GAP + EARLY)
 
         step = tick - AHEAD
 

time: 155 us -> 153 us (0.987)
  Pallas kernels: 155 us -> 153 us
    pallas_call x1, Pallas kernels: 149 us -> 147 us  [body(): pl.pallas_call(kernel, name='correlator', out_shape=pltpu.VMEM((2, CHUNKS...]
where the time goes in v4:
time: 153 us
  Pallas kernels  153 us (100%)
    pallas_call x1, Pallas kernels, body(): pl.pallas_call(kernel, name='correlator', out_shape=pltpu.VMEM((2, CHUNKS...  147 us
    pallas_call x1, Pallas kernels, body(): pl.pallas_call(widen, name='widen', out_shape=jax.ShapeDtypeStruct((2, CH...  6.44 us

profile of v4, /device:TPU:1, one launch (start us, length us, event | category | flops | bytes accessed | tf_op | source)
XLA Modules:
  0.0 153.3 jit_solution(11614431762953821018)
XLA Ops:
  0.0 146.8 %correlator.1.vis = bf16[2,128,32,512]{3,2,1,0:T(8,128)(2,1)S(1)} custom-call(s32[32,32768]{1,0:T(8,128)} %volts.1, s32[32,30720]{1,0:T(8,128)} %hist.1, s32[16,2048]{1,0:T(8,128)} %taps.1, f32[2,1024,128]{2,1,0:T(8,128)} %constant.4.clone.fines, f32[2,16,16,128]{3,2,1,0:T(8,128)} %constant.5.clone.coarses), custom_call_target="tpu_custom_call" | custom-call | tf_op jit(solution)/shard_map/correlator/pallas_call | solution.py:467
  146.8 6.4 %widen.1 = f32[2,128,32,512]{3,2,1,0:T(8,128)} custom-call(bf16[2,128,32,512]{3,2,1,0:T(8,128)(2,1)S(1)} %correlator.1.vis), custom_call_target="tpu_custom_call" | custom-call | tf_op jit(solution)/shard_map/widen/pallas_call | solution.py:510

commit v5 on v4

--- a/solution.py
+++ b/solution.py
@@ -20,7 +20,7 @@
 ROWS = 32
 OWN = ROWS // CHAN
 SLOC = SPEC // CHAN
-RC = 8
+RC = 16
 NR = NT // RC
 CHUNKS = 4
 MIXED = 6
@@ -379,8 +379,9 @@
                         for p in range(2):
                             first_row = p * 128 + to * 32
                             obm[to, p, chunk * MIXED + mixed_at(j) + kk] = vis[first_row : first_row + 32, :]
-                for m in (1, 2, 3):
-                    spread(chunk, j, lax.rem(q + m, 4), q).start()
+                for m in (0, 1):
+                    spread(chunk, j, (1 - x_lo) * 2 + lax.rem(core + m, 2), q).start()
+                spread(chunk, j, x_lo * 2 + 1 - core, q).start()
                 spread_own(chunk, j).start()
 
             @pl.when(is_kept(j))

time: 153 us -> 154 us (level)
  no operation moved by 1% of the time
where the time goes in v5:
time: 154 us
  Pallas kernels  154 us (100%)
    pallas_call x1, Pallas kernels, body(): pl.pallas_call(kernel, name='correlator', out_shape=pltpu.VMEM((2, CHUNKS...  147 us
    pallas_call x1, Pallas kernels, body(): pl.pallas_call(widen, name='widen', out_shape=jax.ShapeDtypeStruct((2, CH...  6.44 us

profile of v5, /device:TPU:1, one launch (start us, length us, event | category | flops | bytes accessed | tf_op | source)
XLA Modules:
  0.0 153.9 jit_solution(7830926879609213601)
XLA Ops:
  0.0 147.5 %correlator.1.vis = bf16[2,128,32,512]{3,2,1,0:T(8,128)(2,1)S(1)} custom-call(s32[32,32768]{1,0:T(8,128)} %volts.1, s32[32,30720]{1,0:T(8,128)} %hist.1, s32[16,2048]{1,0:T(8,128)} %taps.1, f32[2,1024,128]{2,1,0:T(8,128)} %constant.4.clone.fines, f32[2,16,16,128]{3,2,1,0:T(8,128)} %constant.5.clone.coarses), custom_call_target="tpu_custom_call" | custom-call | tf_op jit(solution)/shard_map/correlator/pallas_call | solution.py:468
  147.5 6.4 %widen.1 = f32[2,128,32,512]{3,2,1,0:T(8,128)} custom-call(bf16[2,128,32,512]{3,2,1,0:T(8,128)(2,1)S(1)} %correlator.1.vis), custom_call_target="tpu_custom_call" | custom-call | tf_op jit(solution)/shard_map/widen/pallas_call | solution.py:511
